TPU v7x, 512 devices: a whole 4x4x16 slice. The times are simulated.
512 devices in a mesh: kv: 8 (over x, core), pool: 64 (over y, z).
Axes of the slice: x: 4, y: 4, z: 16, core: 2. Of those that a mesh axis runs over, the one named last changes fastest.
Arguments:
- hidden: bfloat16 [64, 2048], P('pool'), may hold values from -6 to 6
- norm_attn: bfloat16 [2048], replicated, may hold values from 0.099609375 to 1.8984375
- wq: bfloat16 [2048, 2048], P(None, 'kv'), may hold values from -0.125 to 0.125
- wkv: bfloat16 [2, 2048, 1024], P(None, None, 'kv'), may hold values from -0.125 to 0.125
- wo: bfloat16 [2048, 2048], P('kv'), may hold values from -0.125 to 0.125
- cache: bfloat16 [2, 1024, 128, 1024], P(None, 'pool', None, 'kv'), may hold values from -70 to 70, as said below
- slot_entry: int32 [1024], P('pool'), may hold values from -1 to 4095, as said below
- lengths: int32 [64], replicated, may hold values from 1 to 8192, as said below
- norm_mlp: bfloat16 [2048], replicated, may hold values from 0.099609375 to 1.8984375
- w_gate: bfloat16 [2048, 8192], P('pool', 'kv'), may hold values from -0.125 to 0.125
- w_up: bfloat16 [2048, 8192], P('pool', 'kv'), may hold values from -0.125 to 0.125
- w_down: bfloat16 [8192, 2048], P('kv', 'pool'), may hold values from -0.0625 to 0.0625
Outputs:
- output: bfloat16 [64, 2048], P('pool')
Inputs may be any that keep to these rules, and one draw needn't show every extreme that they name: slot_entry[s] is -1 for a free slot, else r * 64 + b: the slot holds block b of request r, that is its cached positions b * 128 to b * 128 + 127 that lie below lengths[r]. Every block of every request below ceil(lengths[r] / 128) sits in exactly one slot, anywhere in the pool; a holder's slots are its 16 entries. Its new token stands at position lengths[r]. `cache`: keys and values of the cached tokens, already rotated.
All inputs are finite; a program needn't handle non-finite values.
Results may differ from a plain program's by a relative error of at most 0.012.
The roundings to bfloat16 on the way count: a program that leaves them out, or rounds other values in their place, can miss the bound.
Values may be sent and summed in bfloat16 or wider, within the bound.
A program may use at most 64 MiB of HBM per device.

v0:
```python
import math
import jax
import jax.numpy as jnp
from jax import lax
from jax.sharding import PartitionSpec as P

QUERY_HEAD_COUNT = 16
KEY_VALUE_HEADS = 8
HEAD_SIZE = 128
NEGATIVE = -1e30
EPSILON = 1e-05
ROPE_BASE = 1000000.0


def combined_all(x, axis, combine):
    everything = jax.tree.map(lambda part: lax.all_gather(part, axis), x)
    initial = jax.tree.map(lambda part: part[0], everything)

    def step(k, so_far):
        return combine(so_far, jax.tree.map(lambda part: part[k], everything))

    return lax.fori_loop(1, lax.axis_size(axis), step, initial)


def narrow_rows(tensor):
    return lax.optimization_barrier(tensor.astype(jnp.bfloat16))


def rms_scale(inputs, gain_vec):
    widened = inputs.astype(jnp.float32)
    mean_square = jnp.mean(widened * widened, axis=-1, keepdims=True)
    return narrow_rows(widened * lax.rsqrt(mean_square + EPSILON) * gain_vec.astype(jnp.float32))


def rotate(vectors, positions):
    head_width = vectors.shape[-1]
    halfway = head_width // 2
    frequency = jnp.exp(
        jnp.arange(halfway, dtype=jnp.float32) * (-2.0 * math.log(ROPE_BASE) / head_width)
    )
    angles = positions.astype(jnp.float32)[:, None] * frequency[None, :]
    cosine = jnp.cos(angles)[:, None, :]
    sine_of = jnp.sin(angles)[:, None, :]
    leading = vectors[..., :halfway]
    trailing = vectors[..., halfway:]
    return jnp.concatenate(
        [leading * cosine - trailing * sine_of, trailing * cosine + leading * sine_of], axis=-1
    )


def combine(earlier, latter):
    highest = jnp.maximum(earlier[0], latter[0])
    scale_early = jnp.exp(earlier[0] - highest)
    scale_late = jnp.exp(latter[0] - highest)
    row_count, head_count = highest.shape
    feature = earlier[2].shape[1] // head_count
    early_out = earlier[2].reshape(row_count, head_count, feature) * scale_early[:, :, None]
    late_out = latter[2].reshape(row_count, head_count, feature) * scale_late[:, :, None]
    weight_sum = earlier[1] * scale_early + latter[1] * scale_late
    return (highest, weight_sum, (early_out + late_out).reshape(row_count, head_count * feature))


def per_device(
    hidden, norm_attn, wq, wkv, wo, cache, slot_entry, lengths, norm_mlp, w_gate, w_up, w_down
):
    home_rows = hidden.shape[0]
    shared_heads = wkv.shape[2] // HEAD_SIZE
    queries_per_shared = QUERY_HEAD_COUNT // KEY_VALUE_HEADS
    query_heads = shared_heads * queries_per_shared
    home_index = lax.axis_index("pool")
    max_blocks = slot_entry.shape[0] * lax.axis_size("pool") // 16
    positions = lax.dynamic_slice_in_dim(lengths, home_index * home_rows, home_rows)
    normed_input = rms_scale(hidden, norm_attn)
    query_rows = jnp.dot(normed_input, wq, preferred_element_type=jnp.float32).reshape(
        home_rows, query_heads, HEAD_SIZE
    )
    query_rows = narrow_rows(rotate(query_rows, positions) * HEAD_SIZE ** (-0.5))
    fresh_keys = jnp.dot(normed_input, wkv[0], preferred_element_type=jnp.float32).reshape(
        home_rows, shared_heads, HEAD_SIZE
    )
    fresh_keys = narrow_rows(rotate(fresh_keys, positions))
    fresh_values = narrow_rows(
        jnp.dot(normed_input, wkv[1], preferred_element_type=jnp.float32)
    ).reshape(home_rows, shared_heads, HEAD_SIZE)
    every_query = lax.all_gather(
        query_rows.reshape(home_rows, query_heads * HEAD_SIZE), "pool", axis=0, tiled=True
    )
    request_list = every_query.shape[0]
    every_query = every_query.reshape(request_list, shared_heads, queries_per_shared, HEAD_SIZE)
    slot_count = slot_entry.shape[0]
    block_len = cache.shape[2]
    live_slot = slot_entry >= 0
    owners = jnp.where(live_slot, slot_entry // max_blocks, 0)
    block_index = jnp.where(live_slot, slot_entry % max_blocks, 0)
    picked = every_query[owners]
    block_keys = cache[0].reshape(slot_count, block_len, shared_heads, HEAD_SIZE)
    block_values = cache[1].reshape(slot_count, block_len, shared_heads, HEAD_SIZE)
    scores = jnp.einsum("sgjd,stgd->sgjt", picked, block_keys, preferred_element_type=jnp.float32)
    position = block_index[:, None] * block_len + jnp.arange(block_len, dtype=jnp.int32)[None, :]
    in_range = live_slot[:, None] & (position < lengths[owners][:, None])
    scores = jnp.where(in_range[:, None, None, :], scores, NEGATIVE)
    block_max = jnp.max(scores, axis=-1)
    same_owner = (owners[:, None] == owners[None, :]) & live_slot[:, None] & live_slot[None, :]
    holder_max = jnp.max(jnp.where(same_owner[:, :, None, None], block_max[None], NEGATIVE), axis=1)
    raised = jnp.where(in_range[:, None, None, :], jnp.exp(scores - holder_max[..., None]), 0.0)
    holder_total = jnp.sum(raised, axis=-1)
    holder_output = jnp.einsum(
        "sgjt,stgd->sgjd", narrow_rows(raised), block_values, preferred_element_type=jnp.float32
    )
    member = (owners[:, None] == jnp.arange(request_list, dtype=jnp.int32)[None, :]) & live_slot[
        :, None
    ]
    request_max = jnp.max(jnp.where(member.T[:, :, None, None], holder_max[None], NEGATIVE), axis=1)
    request_max = request_max.reshape(request_list, query_heads)
    member_float = member.astype(jnp.float32)
    request_total = jnp.einsum(
        "sr,sgj->rgj", member_float, holder_total, precision=lax.Precision.HIGHEST
    )
    request_total = request_total.reshape(request_list, query_heads)
    request_out = jnp.einsum(
        "sr,sgjd->rgjd", member_float, holder_output, precision=lax.Precision.HIGHEST
    )
    request_out = request_out.reshape(request_list, query_heads * HEAD_SIZE)
    merged = combined_all((request_max, request_total, request_out), "pool", combine)
    part_max = lax.dynamic_slice_in_dim(merged[0], home_index * home_rows, home_rows)
    part_total = lax.dynamic_slice_in_dim(merged[1], home_index * home_rows, home_rows)
    part_out = lax.dynamic_slice_in_dim(merged[2], home_index * home_rows, home_rows)
    own_query = query_rows.reshape(home_rows, shared_heads, queries_per_shared, HEAD_SIZE).astype(
        jnp.float32
    )
    new_score = jnp.sum(own_query * fresh_keys.astype(jnp.float32)[:, :, None, :], axis=-1).reshape(
        home_rows, query_heads
    )
    highest = jnp.maximum(part_max, new_score)
    old_scale = jnp.exp(part_max - highest)
    new_scale = jnp.exp(new_score - highest)
    weight_sum = part_total * old_scale + new_scale
    new_term = (
        new_scale.reshape(home_rows, shared_heads, queries_per_shared)[..., None]
        * fresh_values.astype(jnp.float32)[:, :, None, :]
    )
    combined = part_out.reshape(home_rows, query_heads, HEAD_SIZE) * old_scale[
        ..., None
    ] + new_term.reshape(home_rows, query_heads, HEAD_SIZE)
    attended = narrow_rows(combined / weight_sum[..., None]).reshape(
        home_rows, query_heads * HEAD_SIZE
    )
    projected = lax.psum(jnp.dot(attended, wo, preferred_element_type=jnp.float32), "kv")
    residual = narrow_rows(hidden.astype(jnp.float32) + projected)
    mlp_in = rms_scale(residual, norm_mlp)
    columns = lax.all_to_all(mlp_in, "pool", split_axis=1, concat_axis=0, tiled=True)
    hidden_width = w_gate.shape[1]
    gate_term = jnp.dot(columns, w_gate, preferred_element_type=jnp.float32)
    up_term = jnp.dot(columns, w_up, preferred_element_type=jnp.float32)
    summed = lax.psum_scatter(
        jnp.concatenate([gate_term, up_term], axis=1), "pool", scatter_dimension=0, tiled=True
    )
    activation = narrow_rows(jax.nn.silu(summed[:, :hidden_width]) * summed[:, hidden_width:])
    projected_down = jnp.dot(
        lax.all_gather(activation, "pool", axis=0, tiled=True),
        w_down,
        preferred_element_type=jnp.float32,
    )
    mlp_out = narrow_rows(lax.psum(projected_down, "kv"))
    returned = lax.all_to_all(mlp_out, "pool", split_axis=0, concat_axis=1, tiled=True)
    return (residual.astype(jnp.float32) + returned.astype(jnp.float32)).astype(jnp.bfloat16)


def solution(mesh):
    return jax.shard_map(
        per_device,
        mesh=mesh,
        in_specs=(
            P("pool", None),
            P(),
            P(None, "kv"),
            P(None, None, "kv"),
            P("kv", None),
            P(None, "pool", None, "kv"),
            P("pool"),
            P(),
            P(),
            P("pool", "kv"),
            P("pool", "kv"),
            P("kv", "pool"),
        ),
        out_specs=P("pool", None),
        check_vma=False,
    )
```

profile of v0, /device:TPU:8, one launch (start us, length us, event | category | flops | bytes accessed | tf_op | source)
XLA Modules:
  0.0 794.5 jit_solution(5610471597167837660)
XLA Ops:
  8.0 1.2 dynamic_slice.42
  10.6 1.3 multiply_reduce_fusion.1
  13.3 1.5 fusion.5
  15.0 88.2 %all-gather.3 = bf16[64,1,256]{2,1,0:T(2,128)(2,1)S(1)} all-gather(bf16[1,1,256]{2,1,0:T(2,128)(2,1)S(1)} %reshape.618), channel_id=1, replica_groups=mesh['kv'=8,'pool'=64] {'pool'}, dimensions={0}, use_global_device_ids=true | all-gather | bytes 33280 | tf_op jit(solution)/shard_map/all_gather | solution.py:85
  103.4 1.3 gather_fusion
  105.5 1.5 fusion.61
  107.5 1.3 fusion.10
  108.8 0.9 fusion.20
  109.8 1.2 convolution_bitcast_fusion.2
  111.2 1.2 fusion.4
  112.6 79.4 %all-gather.5 = f32[64,64,2]{1,2,0:T(2,128)S(1)} all-gather(f32[1,64,2]{1,2,0:T(2,128)S(1)} %convolution_bitcast_fusion), channel_id=3, replica_groups=mesh['kv'=8,'pool'=64] {'pool'}, dimensions={0}, use_global_device_ids=true | all-gather | bytes 33280 | tf_op jit(solution)/shard_map/all_gather | solution.py:16
  192.2 81.0 %all-gather.4 = f32[64,64,2]{1,2,0:T(2,128)S(1)} all-gather(f32[1,64,2]{1,2,0:T(2,128)S(1)} %bitcast.156), channel_id=2, replica_groups=mesh['kv'=8,'pool'=64] {'pool'}, dimensions={0}, use_global_device_ids=true | all-gather | bytes 33280 | tf_op jit(solution)/shard_map/all_gather | solution.py:16
  274.2 87.2 %while.19 = (s32[]{:T(128)}, f32[64,2]{0,1:T(2,128)S(1)}, f32[64,2]{0,1:T(2,128)S(1)}, f32[64,256]{1,0:T(8,128)S(1)}, f32[64,64,2]{1,2,0:T(2,128)S(1)}, /*index=...) while((s32[]{:T(128)}, f32[64,2]{0,1:T(2,128)S(1)}, ...), condition=%wide.region_6.7_spmd, body=%wide.region_5.6_spmd.sunk | while | flops 49925 | bytes 466071 | solution.py:22
  274.7 0.9 fusion.74
  280.2 0.9 fusion.74
  281.6 0.9 fusion.74
  362.0 12.6 %psum.14 = f32[1,2048]{1,0:T(1,128)S(1)} all-reduce(f32[1,2048]{1,0:T(1,128)S(1)} %fusion.62), channel_id=1, replica_groups=mesh['kv'=8,'pool'=64] {'kv'}, use_global_device_ids=true, to_apply=%region_8.9 | all-reduce | flops 2048 | bytes 16384 | tf_op jit(solution)/shard_map/psum | solution.py:148
  376.2 23.6 %all_to_all.30 = bf16[1,64,32]{2,0,1:T(2,128)(2,1)S(1)} all-to-all(bf16[1,64,32]{2,0,1:T(2,128)(2,1)S(1)} %all_to_all.27), channel_id=1, replica_groups=mesh['kv'=8,'pool'=64] {'pool'}, dimensions={1} | all-to-all | bytes 8192 | tf_op jit(solution)/shard_map/all_to_all | solution.py:151
  401.1 1.3 dynamic-slice
  402.4 255.3 %all-reduce.3.cloned.1.call-done = f32[64,2048]{1,0:T(8,128)} async-done(((f32[64,2048]{1,0:T(8,128)}), f32[64,2048]{1,0:T(8,128)}) %all-reduce.3.cloned.1.call-update) | async-done | bytes 524304
  657.7 1.5 fusion.39
  659.2 80.6 %all-gather.6 = bf16[64,1,1024]{2,1,0:T(2,128)(2,1)S(1)} all-gather(bf16[1,1,1024]{2,1,0:T(2,128)(2,1)S(1)} %bitcast.153), channel_id=1, replica_groups=mesh['kv'=8,'pool'=64] {'pool'}, dimensions={0}, use_global_device_ids=true | all-gather | bytes 133120 | tf_op jit(solution)/shard_map/all_gather | solution.py:160
  739.9 23.6 %psum.15 = bf16[64,32]{0,1:T(8,128)(2,1)S(1)} all-reduce(f32[64,32]{0,1:T(8,128)S(1)} %fusion.17), channel_id=1, replica_groups=mesh['kv'=8,'pool'=64] {'kv'}, use_global_device_ids=true, to_apply=%region_11.12 | all-reduce | flops 2048 | bytes 12288 | tf_op jit(solution)/shard_map/psum | solution.py:164
  763.5 23.4 %all_to_all.31 = bf16[64,1,32]{2,1,0:T(2,128)(2,1)S(1)} all-to-all(bf16[64,1,32]{2,1,0:T(2,128)(2,1)S(1)} %copy.51), channel_id=1, replica_groups=mesh['kv'=8,'pool'=64] {'pool'}, dimensions={0} | all-to-all | bytes 8192 | tf_op jit(solution)/shard_map/all_to_all | solution.py:165
  (443 shorter events, 92.0 us)
Async XLA Ops:
  6.5 355.2 %copy-start = (bf16[256,2048]{1,0:T(8,128)(2,1)S(1)}, bf16[256,2048]{1,0:T(8,128)(2,1)}, u32[]{:S(2)}) copy-start(bf16[256,2048]{1,0:T(8,128)(2,1)} %param.18) | copy-start | bytes 3145732
  6.5 105.9 %copy-start.4 = (bf16[2048]{0:T(1024)(128)(2,1)S(1)}, bf16[2048]{0:T(1024)(128)(2,1)}, u32[]{:S(2)}) copy-start(bf16[2048]{0:T(1024)(128)(2,1)} %param.22) | copy-start | bytes 12292
  6.5 266.8 %all-gather.9.cloned.1.call-start = ((), (), s32[]{:S(2)}) async-start(), calls=%async_computation.2 | async-start | bytes 4259840 | tf_op jit(solution)/shard_map/all_gather | solution.py:16
  14.8 359.9 %copy-start.1 = (bf16[1,2048]{1,0:T(2,128)(2,1)S(1)}, bf16[1,2048]{1,0:T(2,128)(2,1)}, u32[]{:S(2)}) copy-start(bf16[1,2048]{1,0:T(2,128)(2,1)} %param.14) | copy-start | bytes 12292
  15.0 384.8 %copy-start.2 = (bf16[32,1024]{1,0:T(8,128)(2,1)S(1)}, bf16[32,1024]{1,0:T(8,128)(2,1)}, u32[]{:S(2)}) copy-start(bf16[32,1024]{1,0:T(8,128)(2,1)} %param.24) | copy-start | bytes 196612
  103.4 296.6 %copy-start.3 = (bf16[32,1024]{1,0:T(8,128)(2,1)S(1)}, bf16[32,1024]{1,0:T(8,128)(2,1)}, u32[]{:S(2)}) copy-start(bf16[32,1024]{1,0:T(8,128)(2,1)} %param.23) | copy-start | bytes 196612
  109.7 547.9 %all-reduce.3.cloned.1.call-start = ((), (), s32[]{:S(2)}) async-start(), calls=%async_computation.3 | async-start | bytes 1048576
  111.0 628.7 %copy-start.5 = (bf16[1024,32]{0,1:T(8,128)(2,1)S(1)}, bf16[1024,32]{0,1:T(8,128)(2,1)}, u32[]{:S(2)}) copy-start(bf16[1024,32]{0,1:T(8,128)(2,1)} %param.25) | copy-start | bytes 196612
Sparse Core Ops, SparseCore 0:
  109.9 140.5 all-gather.8
  401.2 256.3 all-reduce.2
where the time goes:
time: 798 us; the launch traced here: 795 us
  blocking collectives  412 us (52%)
  waiting for transfers between devices  255 us (32%)
  other arithmetic  66.5 us (8%)
  local copies, waits for them, and re-layouts  33.7 us (4%)
  between operations  15.6 us (2%)
  matrix products  8.65 us (1%)
    unnamed x3, waiting for transfers between devices  255 us
    all_gather x2, blocking collectives, combined_all(): everything = jax.tree.map(lambda part: lax.all_gather(part, axis), x)  160 us
    all_gather x1, blocking collectives, per_device(): lax.all_gather(query_rows.reshape(home_rows, query_heads * HEAD_SIZE), 'p...  88.2 us
    all_gather x1, blocking collectives, per_device(): lax.all_gather(activation, 'pool', axis=0, tiled=True)  80.6 us
    add x63, other arithmetic, combine(): early_out + late_out  55.6 us
    psum x1, blocking collectives, per_device(): mlp_out = narrow_rows(lax.psum(projected_down, 'kv'))  23.6 us
    all_to_all x1, blocking collectives, per_device(): lax.all_to_all(mlp_in, 'pool', split_axis=1, concat_axis=0, tiled=True)  23.6 us
    all_to_all x1, blocking collectives, per_device(): lax.all_to_all(mlp_out, 'pool', split_axis=0, concat_axis=1, tiled=True)  23.4 us
  transfers between devices with their start and end apart: 2, of which 1 were waited for; matrix products, arithmetic and copies ran while one was open for 1% of the time, Pallas kernels for 0%

commit v1 on v0

--- a/solution.py
+++ b/solution.py
@@ -1,3 +1,4 @@
+import functools
 import math
 import jax
 import jax.numpy as jnp
@@ -10,6 +11,19 @@
 NEGATIVE = -1e30
 EPSILON = 1e-05
 ROPE_BASE = 1000000.0
+
+
+def change_the_strips_all(s0, dev_axis):
+    low = lax.all_to_all(
+        jnp.stack(jnp.split(s0, lax.axis_size(dev_axis), axis=0)),
+        axis_name=dev_axis,
+        split_axis=0,
+        concat_axis=0,
+    )
+    return jnp.concatenate(low, axis=1)
+
+
+see_bars = functools.partial(change_the_strips_all, dev_axis="pool")
 
 
 def combined_all(x, axis, combine):
@@ -162,7 +176,7 @@
         preferred_element_type=jnp.float32,
     )
     mlp_out = narrow_rows(lax.psum(projected_down, "kv"))
-    returned = lax.all_to_all(mlp_out, "pool", split_axis=0, concat_axis=1, tiled=True)
+    returned = see_bars(mlp_out)
     return (residual.astype(jnp.float32) + returned.astype(jnp.float32)).astype(jnp.bfloat16)
 
 

time: 798 us -> 800 us (level)
  no operation moved by 1% of the time
where the time goes in v1:
time: 800 us; the launch traced here: 796 us
  blocking collectives  412 us (52%)
  waiting for transfers between devices  255 us (32%)
  other arithmetic  66.5 us (8%)
  local copies, waits for them, and re-layouts  35.6 us (4%)
  between operations  15.8 us (2%)
  matrix products  8.63 us (1%)
    unnamed x3, waiting for transfers between devices  255 us
    all_gather x2, blocking collectives, combined_all(): everything = jax.tree.map(lambda part: lax.all_gather(part, axis), x)  160 us
    all_gather x1, blocking collectives, per_device(): lax.all_gather(query_rows.reshape(home_rows, query_heads * HEAD_SIZE), 'p...  88.2 us
    all_gather x1, blocking collectives, per_device(): lax.all_gather(activation, 'pool', axis=0, tiled=True)  80.6 us
    add x63, other arithmetic, combine(): early_out + late_out  55.6 us
    all_to_all x1, blocking collectives, per_device(): lax.all_to_all(mlp_in, 'pool', split_axis=1, concat_axis=0, tiled=True)  23.6 us
    psum x1, blocking collectives, per_device(): mlp_out = narrow_rows(lax.psum(projected_down, 'kv'))  23.6 us
    all_to_all x1, blocking collectives, change_the_strips_all(): lax.all_to_all(jnp.stack(jnp.split(s0, lax.axis_size(dev_axis), axis=0)),...  23.4 us
  transfers between devices with their start and end apart: 2, of which 1 were waited for; matrix products, arithmetic and copies ran while one was open for 1% of the time, Pallas kernels for 0%

profile of v1, /device:TPU:8, one launch (start us, length us, event | category | flops | bytes accessed | tf_op | source)
XLA Modules:
  0.0 796.4 jit_solution(13739530923830120148)
XLA Ops:
  8.0 1.2 dynamic_slice.42
  10.6 1.3 multiply_reduce_fusion.1
  13.3 1.5 fusion.5
  15.0 88.2 %all-gather.3 = bf16[64,1,256]{2,1,0:T(2,128)(2,1)S(1)} all-gather(bf16[1,1,256]{2,1,0:T(2,128)(2,1)S(1)} %reshape.613), channel_id=1, replica_groups=mesh['kv'=8,'pool'=64] {'pool'}, dimensions={0}, use_global_device_ids=true | all-gather | bytes 33280 | tf_op jit(solution)/shard_map/all_gather | solution.py:99
  103.4 1.3 gather_fusion
  105.5 1.5 fusion.61
  107.5 1.3 fusion.10
  108.8 0.9 fusion.20
  109.8 1.2 convolution_bitcast_fusion.2
  111.2 1.2 fusion.4
  112.6 79.4 %all-gather.5 = f32[64,64,2]{1,2,0:T(2,128)S(1)} all-gather(f32[1,64,2]{1,2,0:T(2,128)S(1)} %convolution_bitcast_fusion), channel_id=3, replica_groups=mesh['kv'=8,'pool'=64] {'pool'}, dimensions={0}, use_global_device_ids=true | all-gather | bytes 33280 | tf_op jit(solution)/shard_map/all_gather | solution.py:30
  192.2 81.0 %all-gather.4 = f32[64,64,2]{1,2,0:T(2,128)S(1)} all-gather(f32[1,64,2]{1,2,0:T(2,128)S(1)} %bitcast.282), channel_id=2, replica_groups=mesh['kv'=8,'pool'=64] {'pool'}, dimensions={0}, use_global_device_ids=true | all-gather | bytes 33280 | tf_op jit(solution)/shard_map/all_gather | solution.py:30
  274.2 87.2 %while.19 = (s32[]{:T(128)}, f32[64,2]{0,1:T(2,128)S(1)}, f32[64,2]{0,1:T(2,128)S(1)}, f32[64,256]{1,0:T(8,128)S(1)}, f32[64,64,2]{1,2,0:T(2,128)S(1)}, /*index=...) while((s32[]{:T(128)}, f32[64,2]{0,1:T(2,128)S(1)}, ...), condition=%wide.region_6.7_spmd, body=%wide.region_5.6_spmd.sunk | while | flops 49925 | bytes 466071 | solution.py:36
  281.6 0.9 fusion.74
  283.0 0.9 fusion.74
  289.9 0.9 fusion.74
  362.0 12.6 %psum.14 = f32[1,2048]{1,0:T(1,128)S(1)} all-reduce(f32[1,2048]{1,0:T(1,128)S(1)} %fusion.62), channel_id=1, replica_groups=mesh['kv'=8,'pool'=64] {'kv'}, use_global_device_ids=true, to_apply=%region_8.9 | all-reduce | flops 2048 | bytes 16384 | tf_op jit(solution)/shard_map/psum | solution.py:162
  376.1 23.6 %all_to_all.22 = bf16[1,64,32]{2,0,1:T(2,128)(2,1)S(1)} all-to-all(bf16[1,64,32]{2,0,1:T(2,128)(2,1)S(1)} %all_to_all.19), channel_id=1, replica_groups=mesh['kv'=8,'pool'=64] {'pool'}, dimensions={1} | all-to-all | bytes 8192 | tf_op jit(solution)/shard_map/all_to_all | solution.py:165
  401.1 1.3 dynamic-slice
  402.3 255.2 %all-reduce.3.cloned.1.call-done = f32[64,2048]{1,0:T(8,128)} async-done(((f32[64,2048]{1,0:T(8,128)}), f32[64,2048]{1,0:T(8,128)}) %all-reduce.3.cloned.1.call-update) | async-done | bytes 524304
  657.6 1.5 fusion.39
  659.1 80.6 %all-gather.6 = bf16[64,1,1024]{2,1,0:T(2,128)(2,1)S(1)} all-gather(bf16[1,1,1024]{2,1,0:T(2,128)(2,1)S(1)} %bitcast.279), channel_id=1, replica_groups=mesh['kv'=8,'pool'=64] {'pool'}, dimensions={0}, use_global_device_ids=true | all-gather | bytes 133120 | tf_op jit(solution)/shard_map/all_gather | solution.py:174
  739.8 23.6 %psum.15 = bf16[64,32]{0,1:T(8,128)(2,1)S(1)} all-reduce(f32[64,32]{0,1:T(8,128)S(1)} %fusion.17), channel_id=1, replica_groups=mesh['kv'=8,'pool'=64] {'kv'}, use_global_device_ids=true, to_apply=%region_11.12 | all-reduce | flops 2048 | bytes 12288 | tf_op jit(solution)/shard_map/psum | solution.py:178
  765.4 23.4 %all_to_all.23 = bf16[64,1,32]{2,1,0:T(2,128)(2,1)S(1)} all-to-all(bf16[64,1,32]{2,1,0:T(2,128)(2,1)S(1)} %constant_dynamic-update-slice_fusion), channel_id=1, replica_groups=mesh['kv'=8,'pool'=64] {'pool'}, dimensions={0} | all-to-all | bytes 8192 | tf_op jit(solution)/shard_map/all_to_all | solution.py:17
  (510 shorter events, 93.8 us)
Async XLA Ops:
  6.5 355.2 %copy-start = (bf16[256,2048]{1,0:T(8,128)(2,1)S(1)}, bf16[256,2048]{1,0:T(8,128)(2,1)}, u32[]{:S(2)}) copy-start(bf16[256,2048]{1,0:T(8,128)(2,1)} %param.18) | copy-start | bytes 3145732
  6.5 105.9 %copy-start.4 = (bf16[2048]{0:T(1024)(128)(2,1)S(1)}, bf16[2048]{0:T(1024)(128)(2,1)}, u32[]{:S(2)}) copy-start(bf16[2048]{0:T(1024)(128)(2,1)} %param.22) | copy-start | bytes 12292
  6.5 266.8 %all-gather.9.cloned.1.call-start = ((), (), s32[]{:S(2)}) async-start(), calls=%async_computation.2 | async-start | bytes 4259840 | tf_op jit(solution)/shard_map/all_gather | solution.py:30
  14.8 359.8 %copy-start.1 = (bf16[1,2048]{1,0:T(2,128)(2,1)S(1)}, bf16[1,2048]{1,0:T(2,128)(2,1)}, u32[]{:S(2)}) copy-start(bf16[1,2048]{1,0:T(2,128)(2,1)} %param.14) | copy-start | bytes 12292
  15.0 384.8 %copy-start.2 = (bf16[32,1024]{1,0:T(8,128)(2,1)S(1)}, bf16[32,1024]{1,0:T(8,128)(2,1)}, u32[]{:S(2)}) copy-start(bf16[32,1024]{1,0:T(8,128)(2,1)} %param.24) | copy-start | bytes 196612
  103.4 296.5 %copy-start.3 = (bf16[32,1024]{1,0:T(8,128)(2,1)S(1)}, bf16[32,1024]{1,0:T(8,128)(2,1)}, u32[]{:S(2)}) copy-start(bf16[32,1024]{1,0:T(8,128)(2,1)} %param.23) | copy-start | bytes 196612
  109.7 547.8 %all-reduce.3.cloned.1.call-start = ((), (), s32[]{:S(2)}) async-start(), calls=%async_computation.3 | async-start | bytes 1048576
  111.0 628.6 %copy-start.5 = (bf16[1024,32]{0,1:T(8,128)(2,1)S(1)}, bf16[1024,32]{0,1:T(8,128)(2,1)}, u32[]{:S(2)}) copy-start(bf16[1024,32]{0,1:T(8,128)(2,1)} %param.25) | copy-start | bytes 196612
Sparse Core Ops, SparseCore 0:
  109.9 140.5 all-gather.8
  401.2 256.3 all-reduce.2
